TPU v7x, 32 devices: a whole 2x2x4 slice. The times are simulated.
32 devices in a mesh: section: 2 (over core), expert: 4 (over z), tensor: 4 (over y, x).
Axes of the slice: x: 2, y: 2, z: 4, core: 2. Of those that a mesh axis runs over, the one named last changes fastest.
Arguments:
- tokens: bfloat16 [32, 197, 768], P('expert'), may hold values from -6 to 6
- batch_order: int32 [4, 8], P('expert'), may hold values from 0 to 7, each once within a row
- gain_attn: float32 [2, 768], P('section'), may hold values from 0.5 to 1.5
- shift_attn: float32 [2, 768], P('section'), may hold values from -3 to 3
- w_qkv: bfloat16 [2, 3, 768, 768], P('section', None, None, 'tensor'), may hold values from -0.21650635 to 0.21650635
- w_out: bfloat16 [2, 768, 768], P('section', 'tensor'), may hold values from -0.875 to 0.875
- gain_moe: float32 [2, 768], P('section'), may hold values from 0.5 to 1.5
- shift_moe: float32 [2, 768], P('section'), may hold values from -3 to 3
- w_router: float32 [2, 768, 8], P('section'), may hold values from -0.04330127 to 0.04330127
- w_in: bfloat16 [2, 8, 768, 3072], P('section', 'expert', None, 'tensor'), may hold values from -0.21875 to 0.21875
- w_back: bfloat16 [2, 8, 3072, 768], P('section', 'expert', 'tensor'), may hold values from -0.4375 to 0.4375
- routes: int32 [2, 32, 197, 2], P('section', 'expert'), may hold values from 0 to 7, as said below
- slots: int32 [2, 32, 197, 2], P('section', 'expert'), may hold values from -1 to 127, as said below
- cotangent: bfloat16 [32, 197, 768], P('expert'), may hold values from -6 to 6
Outputs:
- acts: bfloat16 [2, 32, 197, 768], P('section', 'expert')
- in_grads: float32 [2, 32, 197, 768], P('section', 'expert')
- grad_gain_attn: float32 [2, 768], P('section')
- grad_shift_attn: float32 [2, 768], P('section')
- grad_qkv: float32 [2, 3, 768, 768], P('section', None, None, 'tensor')
- grad_out: float32 [2, 768, 768], P('section', 'tensor')
- grad_gain_moe: float32 [2, 768], P('section')
- grad_shift_moe: float32 [2, 768], P('section')
- grad_router: float32 [2, 768, 8], P('section')
- grad_in: float32 [2, 8, 768, 3072], P('section', 'expert', None, 'tensor')
- grad_back: float32 [2, 8, 3072, 768], P('section', 'expert', 'tensor')
Inputs may be any that keep to these rules, and one draw needn't show every extreme that they name: `routes`: the two experts of a token differ. `slots`: within one layer and one block, choices are ranked first choices by row, then second choices by row, per expert; a choice's slot is its rank, -1 from rank 128 on.
All inputs are finite; a program needn't handle non-finite values.
Results may differ from a plain program's by a relative error of at most 0.019.
Values may be sent and summed in bfloat16 or wider, within the bound.
No kernel may reach another device: no remote copies, remote signals or barrier semaphores. Data moves between devices by JAX's collectives and lax.ppermute only.
A program may use at most 256 MiB of HBM per device.

v0:
```python
import jax
import jax.numpy as jnp
from jax import lax
from jax.sharding import PartitionSpec as P

HEAD = 64
TOPK = 2
SEQ = 197
MB = 4
IMG_MB = 2
NORM_EPS = 1e-06
HIGHEST = lax.Precision.HIGHEST


def from_behind(value, axis, steps):
    count = lax.axis_size(axis)
    first, last = (max(0, -steps), min(count, count - steps))
    return lax.ppermute(value, axis, [(source, source + steps) for source in range(first, last)])


def layer_norm(values, gain, shift):
    centred = values - jnp.mean(values, axis=-1, keepdims=True)
    inverse = lax.rsqrt(jnp.mean(centred * centred, axis=-1, keepdims=True) + NORM_EPS)
    unit_rows = centred * inverse
    return (unit_rows * gain + shift, unit_rows, inverse)


def norm_back(grad, unit_rows, inverse, gain):
    scaled = grad * gain
    inner = (
        scaled
        - jnp.mean(scaled, axis=-1, keepdims=True)
        - unit_rows * jnp.mean(scaled * unit_rows, axis=-1, keepdims=True)
    )
    return (inner * inverse, jnp.sum(grad * unit_rows, axis=0), jnp.sum(grad, axis=0))


def gelu_pair(pre_act):
    normal_cdf = 0.5 * (1.0 + jax.scipy.special.erf(pre_act * 0.7071067811865476))
    density = jnp.exp(-0.5 * pre_act * pre_act) * 0.3989422804014327
    return (pre_act * normal_cdf, normal_cdf + pre_act * density)


def slot_tables(route_block, slot_block, exp_dev, owners, capacity):
    owner_of = route_block // exp_dev
    local_of = route_block % exp_dev
    target = jnp.where(
        slot_block >= 0, local_of * (owners * capacity) + owner_of * capacity + slot_block, -1
    )
    columns = jnp.arange(exp_dev * owners * capacity, dtype=jnp.int32)
    return target[:, :, None] == columns[None, None, :]


def attention_forward(normed_low, wqkv, heads_local, block_rows):
    projected = jnp.einsum(
        "rd,idc->irc", normed_low, wqkv, preferred_element_type=jnp.float32
    ).astype(jnp.bfloat16)
    shaped = projected.reshape(3, IMG_MB, SEQ, heads_local, HEAD)
    scores = jnp.einsum(
        "ishd,ithd->ihst", shaped[0], shaped[1], preferred_element_type=jnp.float32
    ) * HEAD ** (-0.5)
    largest = jnp.max(scores, axis=-1, keepdims=True)
    shifted = jnp.exp(scores - largest)
    row_total = jnp.sum(shifted, axis=-1, keepdims=True)
    attn_probs = (shifted / row_total).astype(jnp.bfloat16)
    mixed_heads = jnp.einsum(
        "ihst,ithd->ishd", attn_probs, shaped[2], preferred_element_type=jnp.float32
    )
    return (
        projected,
        largest + jnp.log(row_total),
        mixed_heads.reshape(block_rows, -1).astype(jnp.bfloat16),
    )


def forward_layer(inputs, weights, route_block, slot_block, layout):
    gain_one, shift_one, wqkv, wout, gain_two, shift_two, wrouter, win, wback = weights
    exp_dev, owners, capacity, heads_local, model_width, block_rows = layout
    normed_a, unit_a, inverse_a = layer_norm(inputs, gain_one, shift_one)
    normed_low = normed_a.astype(jnp.bfloat16)
    projected, logsum, mixed_heads = attention_forward(normed_low, wqkv, heads_local, block_rows)
    attended = lax.psum(jnp.dot(mixed_heads, wout, preferred_element_type=jnp.float32), "tensor")
    hidden = inputs + attended
    normed_m, unit_m, inverse_m = layer_norm(hidden, gain_two, shift_two)
    router_probs = jax.nn.softmax(jnp.dot(normed_m, wrouter, precision=HIGHEST), axis=-1)
    choose = (
        route_block[:, :, None] == jnp.arange(wrouter.shape[1], dtype=jnp.int32)[None, None, :]
    ).astype(jnp.float32)
    gate_values = jnp.sum(router_probs[:, None, :] * choose, axis=-1)
    tables = slot_tables(route_block, slot_block, exp_dev, owners, capacity).astype(jnp.bfloat16)
    sent_rows = jnp.einsum(
        "rks,rd->sd", tables, normed_m.astype(jnp.bfloat16), preferred_element_type=jnp.float32
    ).astype(jnp.bfloat16)
    sent_rows = sent_rows.reshape(exp_dev, owners * capacity, model_width)
    arrived = lax.all_to_all(sent_rows, "expert", split_axis=1, concat_axis=1, tiled=True)
    pre_act = jnp.einsum("erd,edf->erf", arrived, win, preferred_element_type=jnp.float32)
    activated = gelu_pair(pre_act)[0].astype(jnp.bfloat16)
    partial_value = jnp.einsum("erf,efd->erd", activated, wback, preferred_element_type=jnp.float32)
    shares = lax.psum_scatter(partial_value, "tensor", scatter_dimension=2, tiled=True).astype(
        jnp.bfloat16
    )
    quarter = shares.shape[2]
    returned = lax.all_to_all(shares, "expert", split_axis=1, concat_axis=1, tiled=True).reshape(
        -1, quarter
    )
    selected_part = jnp.einsum("rks,sd->rkd", tables, returned, preferred_element_type=jnp.float32)
    hidden_part = lax.dynamic_slice_in_dim(hidden, lax.axis_index("tensor") * quarter, quarter, 1)
    output_part = hidden_part + jnp.sum(gate_values[:, :, None] * selected_part, axis=1)
    output, selected = (
        lax.all_gather(output_part, "tensor", axis=1, tiled=True),
        lax.all_gather(selected_part, "tensor", axis=2, tiled=True),
    )
    saved = (
        unit_a,
        inverse_a,
        normed_low,
        projected,
        logsum,
        mixed_heads,
        unit_m,
        inverse_m,
        normed_m,
        router_probs,
        choose,
        gate_values,
        tables,
        arrived,
        pre_act,
        selected,
    )
    return (output, saved)


def backward_layer(grad_output, weights, saved, layout):
    gain_one, shift_one, wqkv, wout, gain_two, shift_two, wrouter, win, wback = weights
    exp_dev, owners, capacity, heads_local, model_width, block_rows = layout
    (
        unit_a,
        inverse_a,
        normed_low,
        projected,
        logsum,
        mixed_heads,
        unit_m,
        inverse_m,
        normed_m,
        router_probs,
        choose,
        gate_values,
        tables,
        arrived,
        pre_act,
        selected,
    ) = saved
    grad_gates = jnp.sum(grad_output[:, None, :] * selected, axis=-1)
    activated, slope = gelu_pair(pre_act)
    quarter = model_width // lax.axis_size("tensor")
    grad_part = lax.dynamic_slice_in_dim(
        grad_output, lax.axis_index("tensor") * quarter, quarter, 1
    )
    weighted = (gate_values[:, :, None] * grad_part[:, None, :]).astype(jnp.bfloat16)
    grad_sent = jnp.einsum(
        "rks,rkd->sd", tables, weighted, preferred_element_type=jnp.float32
    ).astype(jnp.bfloat16)
    arrived_part = lax.all_to_all(
        grad_sent.reshape(exp_dev, owners * capacity, quarter),
        "expert",
        split_axis=1,
        concat_axis=1,
        tiled=True,
    )
    grad_arrived = lax.all_gather(arrived_part, "tensor", axis=2, tiled=True)
    grad_wback = jnp.einsum(
        "erf,erd->efd",
        activated.astype(jnp.bfloat16),
        grad_arrived,
        preferred_element_type=jnp.float32,
    )
    grad_pre = (
        jnp.einsum("erd,efd->erf", grad_arrived, wback, preferred_element_type=jnp.float32) * slope
    ).astype(jnp.bfloat16)
    grad_win = jnp.einsum("erd,erf->edf", arrived, grad_pre, preferred_element_type=jnp.float32)
    row_terms = jnp.einsum("erf,edf->erd", grad_pre, win, preferred_element_type=jnp.float32)
    grad_share = lax.psum_scatter(row_terms, "tensor", scatter_dimension=2, tiled=True).astype(
        jnp.bfloat16
    )
    home_part = lax.all_to_all(grad_share, "expert", split_axis=1, concat_axis=1, tiled=True)
    grad_home = lax.all_gather(home_part, "tensor", axis=2, tiled=True).reshape(-1, model_width)
    grad_norm_m = jnp.einsum("rks,sd->rd", tables, grad_home, preferred_element_type=jnp.float32)
    grad_probs = jnp.sum(choose * grad_gates[:, :, None], axis=1)
    grad_logits = router_probs * (
        grad_probs - jnp.sum(router_probs * grad_probs, axis=-1, keepdims=True)
    )
    grad_wrouter = jnp.einsum("rd,re->de", normed_m, grad_logits, precision=HIGHEST)
    grad_norm_m = grad_norm_m + jnp.einsum("re,de->rd", grad_logits, wrouter, precision=HIGHEST)
    grad_hidden_ln, grad_gain_two, grad_shift_two = norm_back(
        grad_norm_m, unit_m, inverse_m, gain_two
    )
    grad_hidden = grad_output + grad_hidden_ln
    grad_attn_low = grad_hidden.astype(jnp.bfloat16)
    grad_wout = jnp.einsum(
        "rc,rd->cd", mixed_heads, grad_attn_low, preferred_element_type=jnp.float32
    )
    grad_mixed = jnp.einsum(
        "rd,cd->rc", grad_attn_low, wout, preferred_element_type=jnp.float32
    ).astype(jnp.bfloat16)
    shaped = projected.reshape(3, IMG_MB, SEQ, heads_local, HEAD)
    score_scale = HEAD ** (-0.5)
    scores = (
        jnp.einsum("ishd,ithd->ihst", shaped[0], shaped[1], preferred_element_type=jnp.float32)
        * score_scale
    )
    attn_probs = jnp.exp(scores - logsum)
    grad_heads = grad_mixed.reshape(IMG_MB, SEQ, heads_local, HEAD)
    grad_values = jnp.einsum(
        "ihst,ishd->ithd",
        attn_probs.astype(jnp.bfloat16),
        grad_heads,
        preferred_element_type=jnp.float32,
    )
    grad_weights_soft = jnp.einsum(
        "ishd,ithd->ihst", grad_heads, shaped[2], preferred_element_type=jnp.float32
    )
    grad_scores = (
        attn_probs
        * (grad_weights_soft - jnp.sum(attn_probs * grad_weights_soft, axis=-1, keepdims=True))
    ).astype(jnp.bfloat16)
    grad_queries = (
        jnp.einsum("ihst,ithd->ishd", grad_scores, shaped[1], preferred_element_type=jnp.float32)
        * score_scale
    )
    grad_keys = (
        jnp.einsum("ihst,ishd->ithd", grad_scores, shaped[0], preferred_element_type=jnp.float32)
        * score_scale
    )
    grad_projected = (
        jnp.stack([grad_queries, grad_keys, grad_values])
        .reshape(3, block_rows, -1)
        .astype(jnp.bfloat16)
    )
    grad_wqkv = jnp.einsum(
        "rd,irc->idc", normed_low, grad_projected, preferred_element_type=jnp.float32
    )
    grad_normed_a = lax.psum(
        jnp.einsum("irc,idc->rd", grad_projected, wqkv, preferred_element_type=jnp.float32),
        "tensor",
    )
    grad_input_ln, grad_gain_one, grad_shift_one = norm_back(
        grad_normed_a, unit_a, inverse_a, gain_one
    )
    grad_input = grad_hidden + grad_input_ln
    return (
        grad_input,
        (
            grad_gain_one,
            grad_shift_one,
            grad_wqkv,
            grad_wout,
            grad_gain_two,
            grad_shift_two,
            grad_wrouter,
            grad_win,
            grad_wback,
        ),
    )


def shards(
    tokens,
    batch_order,
    gain_attn,
    shift_attn,
    w_qkv,
    w_out,
    gain_moe,
    shift_moe,
    w_router,
    w_in,
    w_back,
    routes,
    slots,
    cotangent,
):
    section_index = lax.axis_index("section")
    section_count = lax.axis_size("section")
    owners = lax.axis_size("expert")
    exp_dev = w_in.shape[1]
    experts = exp_dev * owners
    model_width = tokens.shape[2]
    block_rows = IMG_MB * SEQ
    capacity = (TOPK * block_rows * 5 // (4 * experts) + 7) // 8 * 8
    heads_local = w_qkv.shape[3] // HEAD
    layout = (exp_dev, owners, capacity, heads_local, model_width, block_rows)
    tick_count = MB + section_count - 1
    image_order = batch_order[0]
    weights = (
        gain_attn[0],
        shift_attn[0],
        w_qkv[0],
        w_out[0],
        gain_moe[0],
        shift_moe[0],
        w_router[0],
        w_in[0],
        w_back[0],
    )
    route_blocks = routes[0].reshape(MB, block_rows, TOPK)
    slot_blocks = slots[0].reshape(MB, block_rows, TOPK)
    inbound = jnp.zeros((block_rows, model_width), jnp.bfloat16)
    acts_store = jnp.zeros((MB, block_rows, model_width), jnp.bfloat16)
    kept_ticks = []
    for tick_index in range(tick_count):
        micro_index = tick_index - section_index
        active = (micro_index >= 0) & (micro_index < MB)
        clipped = jnp.clip(micro_index, 0, MB - 1)
        if tick_index < MB:
            fresh = jnp.take(
                tokens, image_order[tick_index * IMG_MB : (tick_index + 1) * IMG_MB], axis=0
            ).reshape(block_rows, model_width)
        else:
            fresh = jnp.zeros((block_rows, model_width), jnp.bfloat16)
        inputs = jnp.where(section_index == 0, fresh, inbound).astype(jnp.float32)
        route_block = lax.dynamic_index_in_dim(route_blocks, clipped, 0, keepdims=False)
        slot_block = lax.dynamic_index_in_dim(slot_blocks, clipped, 0, keepdims=False)
        output, saved = forward_layer(inputs, weights, route_block, slot_block, layout)
        output_low = output.astype(jnp.bfloat16)
        previous = lax.dynamic_index_in_dim(acts_store, clipped, 0, keepdims=False)
        acts_store = lax.dynamic_update_index_in_dim(
            acts_store, jnp.where(active, output_low, previous), clipped, 0
        )
        kept_ticks.append((saved, active, clipped))
        if tick_index + 1 < tick_count:
            inbound = from_behind(output_low, "section", 1)
    targets = jnp.take(cotangent, image_order, axis=0).reshape(MB, block_rows, model_width)
    grad_inbound = jnp.zeros((block_rows, model_width), jnp.bfloat16)
    grad_store = jnp.zeros((MB, block_rows, model_width), jnp.float32)
    totals = tuple((jnp.zeros(weight_item.shape, jnp.float32) for weight_item in weights))
    for back_index in range(tick_count):
        saved, active, clipped = kept_ticks[tick_count - 1 - back_index]
        target_rows = lax.dynamic_index_in_dim(targets, clipped, 0, keepdims=False)
        grad_output = jnp.where(
            section_index == section_count - 1, target_rows, grad_inbound
        ).astype(jnp.float32)
        grad_input, layer_grads = backward_layer(grad_output, weights, saved, layout)
        totals = tuple(
            (
                running + jnp.where(active, fresh_grad, 0.0)
                for running, fresh_grad in zip(totals, layer_grads)
            )
        )
        previous = lax.dynamic_index_in_dim(grad_store, clipped, 0, keepdims=False)
        grad_store = lax.dynamic_update_index_in_dim(
            grad_store, jnp.where(active, grad_input, previous), clipped, 0
        )
        if back_index + 1 < tick_count:
            grad_inbound = from_behind(grad_input.astype(jnp.bfloat16), "section", -1)
    shared = lax.psum(
        (totals[0], totals[1], totals[2], totals[3], totals[4], totals[5], totals[6]), "expert"
    )
    image_count = MB * IMG_MB
    acts_image = (
        jnp.zeros((image_count, SEQ, model_width), jnp.bfloat16)
        .at[image_order]
        .set(acts_store.reshape(image_count, SEQ, model_width))
    )
    grads_image = (
        jnp.zeros((image_count, SEQ, model_width), jnp.float32)
        .at[image_order]
        .set(grad_store.reshape(image_count, SEQ, model_width))
    )
    return (
        acts_image[None],
        grads_image[None],
        shared[0][None],
        shared[1][None],
        shared[2][None],
        shared[3][None],
        shared[4][None],
        shared[5][None],
        shared[6][None],
        totals[7][None],
        totals[8][None],
    )


def solution(mesh):
    return jax.shard_map(
        shards,
        mesh=mesh,
        in_specs=(
            P("expert", None, None),
            P("expert", None),
            P("section", None),
            P("section", None),
            P("section", None, None, "tensor"),
            P("section", "tensor", None),
            P("section", None),
            P("section", None),
            P("section", None, None),
            P("section", "expert", None, "tensor"),
            P("section", "expert", "tensor", None),
            P("section", "expert", None, None),
            P("section", "expert", None, None),
            P("expert", None, None),
        ),
        out_specs=(
            P("section", "expert", None, None),
            P("section", "expert", None, None),
            P("section", None),
            P("section", None),
            P("section", None, None, "tensor"),
            P("section", "tensor", None),
            P("section", None),
            P("section", None),
            P("section", None, None),
            P("section", "expert", None, "tensor"),
            P("section", "expert", "tensor", None),
        ),
        check_vma=False,
    )
```

profile of v0, /device:TPU:0, one launch (start us, length us, event | category | flops | bytes accessed | tf_op | source)
XLA Modules:
  0.0 2706.1 jit_solution(5228686551862741128)
XLA Ops:
  36.3 55.6 %all-reduce.14.cloned.1.call-done = f32[394,768]{0,1:T(8,128)} async-done(((f32[394,768]{0,1:T(8,128)}), f32[394,768]{0,1:T(8,128)}) %all-reduce.14.cloned.1.call-update) | async-done | bytes 1210384 | tf_op jit(solution)/shard_map/psum | solution.py:82
  98.9 41.3 %all_to_all.100 = bf16[2,512,768]{2,0,1:T(2,128)(2,1)} all-to-all(bf16[2,512,768]{2,0,1:T(2,128)(2,1)S(1)} %copy.1194), channel_id=1, replica_groups=mesh['section'=2,'expert'=4,'tensor'=4] {'expert'}, dimensions={1} | all-to-all | bytes 3145728 | tf_op jit(solution)/shard_map/all_to_all | solution.py:95
  153.5 42.1 %reduce-scatter.11.cloned.1.call-done = f32[2,512,192]{1,2,0:T(8,128)} async-done(((f32[2,512,768]{1,2,0:T(8,128)}), f32[2,512,192]{1,2,0:T(8,128)}) %reduce-scatter.11.cloned.1.call-update) | async-done | bytes 786448 | tf_op jit(solution)/shard_map/reduce_scatter | solution.py:99
  272.3 57.2 %all-reduce.16.cloned.1.call-done = f32[394,768]{0,1:T(8,128)} async-done(((f32[394,768]{0,1:T(8,128)}), f32[394,768]{0,1:T(8,128)}) %all-reduce.16.cloned.1.call-update) | async-done | bytes 1210384 | tf_op jit(solution)/shard_map/psum | solution.py:82
  336.0 41.3 %all_to_all.101 = bf16[2,512,768]{2,0,1:T(2,128)(2,1)} all-to-all(bf16[2,512,768]{2,0,1:T(2,128)(2,1)S(1)} %copy.1211), channel_id=1, replica_groups=mesh['section'=2,'expert'=4,'tensor'=4] {'expert'}, dimensions={1} | all-to-all | bytes 3145728 | tf_op jit(solution)/shard_map/all_to_all | solution.py:95
  392.2 42.2 %reduce-scatter.13.cloned.1.call-done = f32[2,512,192]{1,2,0:T(8,128)} async-done(((f32[2,512,768]{1,2,0:T(8,128)}), f32[2,512,192]{1,2,0:T(8,128)}) %reduce-scatter.13.cloned.1.call-update) | async-done | bytes 786448 | tf_op jit(solution)/shard_map/reduce_scatter | solution.py:99
  503.5 58.1 %all-reduce.18.cloned.1.call-done = f32[394,768]{0,1:T(8,128)} async-done(((f32[394,768]{0,1:T(8,128)}), f32[394,768]{0,1:T(8,128)}) %all-reduce.18.cloned.1.call-update) | async-done | bytes 1210384 | tf_op jit(solution)/shard_map/psum | solution.py:82
  568.0 41.3 %all_to_all.102 = bf16[2,512,768]{2,0,1:T(2,128)(2,1)} all-to-all(bf16[2,512,768]{2,0,1:T(2,128)(2,1)S(1)} %copy.1229), channel_id=1, replica_groups=mesh['section'=2,'expert'=4,'tensor'=4] {'expert'}, dimensions={1} | all-to-all | bytes 3145728 | tf_op jit(solution)/shard_map/all_to_all | solution.py:95
  624.3 42.2 %reduce-scatter.15.cloned.1.call-done = f32[2,512,192]{1,2,0:T(8,128)} async-done(((f32[2,512,768]{1,2,0:T(8,128)}), f32[2,512,192]{1,2,0:T(8,128)}) %reduce-scatter.15.cloned.1.call-update) | async-done | bytes 786448 | tf_op jit(solution)/shard_map/reduce_scatter | solution.py:99
  715.2 58.7 %all-reduce.20.cloned.1.call-done = f32[394,768]{0,1:T(8,128)} async-done(((f32[394,768]{0,1:T(8,128)}), f32[394,768]{0,1:T(8,128)}) %all-reduce.20.cloned.1.call-update) | async-done | bytes 1210384 | tf_op jit(solution)/shard_map/psum | solution.py:82
  780.3 41.5 %all_to_all.103 = bf16[2,512,768]{2,0,1:T(2,128)(2,1)} all-to-all(bf16[2,512,768]{2,0,1:T(2,128)(2,1)S(1)} %copy.1247), channel_id=1, replica_groups=mesh['section'=2,'expert'=4,'tensor'=4] {'expert'}, dimensions={1} | all-to-all | bytes 3145728 | tf_op jit(solution)/shard_map/all_to_all | solution.py:95
  836.7 42.2 %reduce-scatter.17.cloned.1.call-done = f32[2,512,192]{1,2,0:T(8,128)} async-done(((f32[2,512,768]{1,2,0:T(8,128)}), f32[2,512,192]{1,2,0:T(8,128)}) %reduce-scatter.17.cloned.1.call-update) | async-done | bytes 786448 | tf_op jit(solution)/shard_map/reduce_scatter | solution.py:99
  925.6 58.5 %all-reduce.22.cloned.1.call-done = f32[394,768]{0,1:T(8,128)} async-done(((f32[394,768]{0,1:T(8,128)}), f32[394,768]{0,1:T(8,128)}) %all-reduce.22.cloned.1.call-update) | async-done | bytes 1210384 | tf_op jit(solution)/shard_map/psum | solution.py:82
  1043.9 42.1 %reduce-scatter.19.cloned.1.call-done = f32[2,512,192]{1,2,0:T(8,128)} async-done(((f32[2,512,768]{1,2,0:T(8,128)}), f32[2,512,192]{1,2,0:T(8,128)}) %reduce-scatter.19.cloned.1.call-update) | async-done | bytes 786448 | tf_op jit(solution)/shard_map/reduce_scatter | solution.py:99
  1220.5 44.0 %reduce-scatter.21.cloned.1.call-done = f32[2,512,192]{1,2,0:T(8,128)} async-done(((f32[2,512,768]{1,2,0:T(8,128)}), f32[2,512,192]{1,2,0:T(8,128)}) %reduce-scatter.21.cloned.1.call-update) | async-done | bytes 786448 | tf_op jit(solution)/shard_map/reduce_scatter | solution.py:184
  1338.4 60.8 %all-reduce.24.cloned.1.call-done = f32[394,768]{0,1:T(8,128)} async-done(((f32[394,768]{0,1:T(8,128)}), f32[394,768]{0,1:T(8,128)}) %all-reduce.24.cloned.1.call-update) | async-done | bytes 1210384 | tf_op jit(solution)/shard_map/psum | solution.py:244
  1476.1 43.4 %reduce-scatter.23.cloned.1.call-done = f32[2,512,192]{1,2,0:T(8,128)} async-done(((f32[2,512,768]{1,2,0:T(8,128)}), f32[2,512,192]{1,2,0:T(8,128)}) %reduce-scatter.23.cloned.1.call-update) | async-done | bytes 786448 | tf_op jit(solution)/shard_map/reduce_scatter | solution.py:184
  1624.9 52.6 %all-reduce.26.cloned.1.call-done = f32[394,768]{0,1:T(8,128)} async-done(((f32[394,768]{0,1:T(8,128)}), f32[394,768]{0,1:T(8,128)}) %all-reduce.26.cloned.1.call-update) | async-done | bytes 1210384 | tf_op jit(solution)/shard_map/psum | solution.py:244
  1756.4 43.3 %reduce-scatter.25.cloned.1.call-done = f32[2,512,192]{1,2,0:T(8,128)} async-done(((f32[2,512,768]{1,2,0:T(8,128)}), f32[2,512,192]{1,2,0:T(8,128)}) %reduce-scatter.25.cloned.1.call-update) | async-done | bytes 786448 | tf_op jit(solution)/shard_map/reduce_scatter | solution.py:184
  1905.2 52.5 %all-reduce.28.cloned.1.call-done = f32[394,768]{0,1:T(8,128)} async-done(((f32[394,768]{0,1:T(8,128)}), f32[394,768]{0,1:T(8,128)}) %all-reduce.28.cloned.1.call-update) | async-done | bytes 1210384 | tf_op jit(solution)/shard_map/psum | solution.py:244
  2036.5 43.3 %reduce-scatter.27.cloned.1.call-done = f32[2,512,192]{1,2,0:T(8,128)} async-done(((f32[2,512,768]{1,2,0:T(8,128)}), f32[2,512,192]{1,2,0:T(8,128)}) %reduce-scatter.27.cloned.1.call-update) | async-done | bytes 786448 | tf_op jit(solution)/shard_map/reduce_scatter | solution.py:184
  2198.3 49.9 %all-reduce.30.cloned.1.call-done = f32[394,768]{0,1:T(8,128)} async-done(((f32[394,768]{0,1:T(8,128)}), f32[394,768]{0,1:T(8,128)}) %all-reduce.30.cloned.1.call-update) | async-done | bytes 1210384 | tf_op jit(solution)/shard_map/psum | solution.py:244
  2554.9 41.4 %all-reduce.32.cloned.1.call-done = f32[394,768]{0,1:T(8,128)} async-done(((f32[394,768]{0,1:T(8,128)}), f32[394,768]{0,1:T(8,128)}) %all-reduce.32.cloned.1.call-update) | async-done | bytes 1210384 | tf_op jit(solution)/shard_map/psum | solution.py:244
  2649.5 45.8 %all-reduce.34.cloned.1.call-done = (f32[1,3,768,192]{2,3,1,0:T(8,128)}, f32[1,192,768]{2,1,0:T(8,128)}) async-done(((f32[1,3,768,192]{2,3,1,0:T(8,128)}, f32[1,192,768]{2,1,0:T(8,128)}), (f32[1,3,768,192]{2,3,1,0:T(8,128)}, f32[1,192,768]{2,1,0:T(8,128)})) %all-reduce.34.cloned.1.call-update) | async-done | bytes 2359312 | tf_op jit(solution)/shard_map/psum | solution.py:357
  (1442 shorter events, 1544.8 us)
Async XLA Ops:
  28.2 167.4 %reduce-scatter.11.cloned.1.call-start = ((), (), s32[]{:S(2)}) async-start(), calls=%async_computation.31 | async-start | bytes 3932160 | tf_op jit(solution)/shard_map/reduce_scatter | solution.py:99
  202.5 127.0 %all-reduce.16.cloned.1.call-start = ((), (), s32[]{:S(2)}) async-start(), calls=%async_computation.32 | async-start | bytes 3145728 | tf_op jit(solution)/shard_map/psum | solution.py:82
  270.1 164.3 %reduce-scatter.13.cloned.1.call-start = ((), (), s32[]{:S(2)}) async-start(), calls=%async_computation.33 | async-start | bytes 3932160 | tf_op jit(solution)/shard_map/reduce_scatter | solution.py:99
  441.2 120.3 %all-reduce.18.cloned.1.call-start = ((), (), s32[]{:S(2)}) async-start(), calls=%async_computation.34 | async-start | bytes 3145728 | tf_op jit(solution)/shard_map/psum | solution.py:82
  502.1 164.3 %reduce-scatter.15.cloned.1.call-start = ((), (), s32[]{:S(2)}) async-start(), calls=%async_computation.35 | async-start | bytes 3932160 | tf_op jit(solution)/shard_map/reduce_scatter | solution.py:99
  673.3 100.6 %all-reduce.20.cloned.1.call-start = ((), (), s32[]{:S(2)}) async-start(), calls=%async_computation.36 | async-start | bytes 3145728 | tf_op jit(solution)/shard_map/psum | solution.py:82
  713.9 165.0 %reduce-scatter.17.cloned.1.call-start = ((), (), s32[]{:S(2)}) async-start(), calls=%async_computation.37 | async-start | bytes 3932160 | tf_op jit(solution)/shard_map/reduce_scatter | solution.py:99
  924.7 161.3 %reduce-scatter.19.cloned.1.call-start = ((), (), s32[]{:S(2)}) async-start(), calls=%async_computation.39 | async-start | bytes 3932160 | tf_op jit(solution)/shard_map/reduce_scatter | solution.py:99
  1043.8 109.5 %all-gather.20.cloned.1.call-start = ((), (), s32[]{:S(2)}) async-start(), calls=%async_computation.43 | async-start | bytes 3932160 | tf_op jit(solution)/shard_map/all_gather | solution.py:111
  1290.1 109.1 %all-reduce.24.cloned.1.call-start = ((), (), s32[]{:S(2)}) async-start(), calls=%async_computation.44 | async-start | bytes 3145728 | tf_op jit(solution)/shard_map/psum | solution.py:244
  1338.3 127.4 %all-gather.22.cloned.1.call-start = ((), (), s32[]{:S(2)}) async-start(), calls=%async_computation.45 | async-start | bytes 1966080 | tf_op jit(solution)/shard_map/all_gather | solution.py:172
  1476.1 122.3 %all-gather.24.cloned.1.call-start = ((), (), s32[]{:S(2)}) async-start(), calls=%async_computation.47 | async-start | bytes 1966080 | tf_op jit(solution)/shard_map/all_gather | solution.py:188
  1545.1 132.5 %all-reduce.26.cloned.1.call-start = ((), (), s32[]{:S(2)}) async-start(), calls=%async_computation.49 | async-start | bytes 3145728 | tf_op jit(solution)/shard_map/psum | solution.py:244
  1616.7 129.2 %all-gather.28.cloned.1.call-start = ((), (), s32[]{:S(2)}) async-start(), calls=%async_computation.50 | async-start | bytes 1966080 | tf_op jit(solution)/shard_map/all_gather | solution.py:172
  1756.4 122.2 %all-gather.30.cloned.1.call-start = ((), (), s32[]{:S(2)}) async-start(), calls=%async_computation.52 | async-start | bytes 1966080 | tf_op jit(solution)/shard_map/all_gather | solution.py:188
  1825.3 132.4 %all-reduce.28.cloned.1.call-start = ((), (), s32[]{:S(2)}) async-start(), calls=%async_computation.54 | async-start | bytes 3145728 | tf_op jit(solution)/shard_map/psum | solution.py:244
  1896.8 129.2 %all-gather.34.cloned.1.call-start = ((), (), s32[]{:S(2)}) async-start(), calls=%async_computation.55 | async-start | bytes 1966080 | tf_op jit(solution)/shard_map/all_gather | solution.py:172
  2036.5 122.3 %all-gather.36.cloned.1.call-start = ((), (), s32[]{:S(2)}) async-start(), calls=%async_computation.57 | async-start | bytes 1966080 | tf_op jit(solution)/shard_map/all_gather | solution.py:188
  2105.4 142.8 %all-reduce.30.cloned.1.call-start = ((), (), s32[]{:S(2)}) async-start(), calls=%async_computation.59 | async-start | bytes 3145728 | tf_op jit(solution)/shard_map/psum | solution.py:244
  2187.3 136.5 %all-gather.40.cloned.1.call-start = ((), (), s32[]{:S(2)}) async-start(), calls=%async_computation.60 | async-start | bytes 1966080 | tf_op jit(solution)/shard_map/all_gather | solution.py:172
  2294.7 165.7 %reduce-scatter.29.cloned.1.call-start = ((), (), s32[]{:S(2)}) async-start(), calls=%async_computation.61 | async-start | bytes 3932160 | tf_op jit(solution)/shard_map/reduce_scatter | solution.py:184
  2333.7 148.8 %all-gather.44.cloned.1.call-start = ((), (), s32[]{:S(2)}) async-start(), calls=%async_computation.63 | async-start | bytes 3932160 | tf_op jit(solution)/shard_map/all_gather | solution.py:111
  2482.2 114.1 %all-reduce.32.cloned.1.call-start = ((), (), s32[]{:S(2)}) async-start(), calls=%async_computation.64 | async-start | bytes 3145728 | tf_op jit(solution)/shard_map/psum | solution.py:244
  2535.4 159.9 %all-reduce.34.cloned.1.call-start = ((), (), s32[]{:S(2)}) async-start(), calls=%async_computation.65 | async-start | bytes 4718592 | tf_op jit(solution)/shard_map/psum | solution.py:357
  (406 other events, 7731.0 us)
Sparse Core Ops, SparseCore 0:
  28.3 63.4 all-reduce.13
  153.5 42.0 reduce-scatter.10
  270.2 59.2 all-reduce.15
  392.3 42.0 reduce-scatter.12
  502.2 59.2 all-reduce.17
  624.4 42.0 reduce-scatter.14
  714.0 59.8 all-reduce.19
  836.8 42.0 reduce-scatter.16
  924.8 59.2 all-reduce.21
  1220.6 43.8 reduce-scatter.20
  1338.4 60.7 all-reduce.23
  1475.6 43.8 reduce-scatter.22
  1521.2 43.8 all-gather.25
  1616.8 60.7 all-reduce.25
  1755.8 43.8 reduce-scatter.24
  1801.6 43.8 all-gather.31
  1896.9 60.7 all-reduce.27
  2035.9 43.8 reduce-scatter.26
  2081.6 43.8 all-gather.37
  2187.4 60.7 all-reduce.29
  2333.8 43.8 reduce-scatter.28
  2379.4 45.9 all-gather.43
  2535.5 60.7 all-reduce.31
  2599.1 96.1 all-reduce.33
  (12 shorter events, 381.0 us)
where the time goes:
time: 2720 us; the launch traced here: 2710 us
  waiting for transfers between devices  1370 us (50%)
  blocking collectives  482 us (18%)
  local copies, waits for them, and re-layouts  397 us (15%)
  matrix products  269 us (10%)
  other arithmetic  125 us (5%)
  starting transfers between devices  39.8 us (1%)
    psum x5, waiting for transfers between devices, forward_layer(): lax.psum(jnp.dot(mixed_heads, wout, preferred_element_type=jnp.float32),...  288 us
    psum x5, waiting for transfers between devices, backward_layer(): lax.psum(jnp.einsum('irc,idc->rd', grad_projected, wqkv, preferred_elemen...  257 us
    reduce_scatter x5, waiting for transfers between devices, forward_layer(): lax.psum_scatter(partial_value, 'tensor', scatter_dimension=2, tiled=True)  211 us
    all_to_all x5, blocking collectives, forward_layer(): lax.all_to_all(sent_rows, 'expert', split_axis=1, concat_axis=1, tiled=True)  207 us
    reduce_scatter x5, waiting for transfers between devices, backward_layer(): lax.psum_scatter(row_terms, 'tensor', scatter_dimension=2, tiled=True)  174 us
    all_gather x5, waiting for transfers between devices, backward_layer(): grad_arrived = lax.all_gather(arrived_part, 'tensor', axis=2, tiled=True)  145 us
    all_gather x5, waiting for transfers between devices, backward_layer(): lax.all_gather(home_part, 'tensor', axis=2, tiled=True)  120 us
    all_to_all x5, blocking collectives, backward_layer(): lax.all_to_all(grad_sent.reshape(exp_dev, owners * capacity, quarter), 'e...  96 us
  transfers between devices with their start and end apart: 49, of which 43 were waited for; matrix products, arithmetic and copies ran while one was open for 12% of the time, Pallas kernels for 0%

commit v1 on v0

--- a/solution.py
+++ b/solution.py
@@ -79,7 +79,10 @@
     normed_a, unit_a, inverse_a = layer_norm(inputs, gain_one, shift_one)
     normed_low = normed_a.astype(jnp.bfloat16)
     projected, logsum, mixed_heads = attention_forward(normed_low, wqkv, heads_local, block_rows)
-    attended = lax.psum(jnp.dot(mixed_heads, wout, preferred_element_type=jnp.float32), "tensor")
+    attended = jnp.sum(
+        lax.all_gather(jnp.dot(mixed_heads, wout, preferred_element_type=jnp.float32), "tensor"),
+        axis=0,
+    )
     hidden = inputs + attended
     normed_m, unit_m, inverse_m = layer_norm(hidden, gain_two, shift_two)
     router_probs = jax.nn.softmax(jnp.dot(normed_m, wrouter, precision=HIGHEST), axis=-1)

time: 2720 us -> 2720 us (level)
    psum x5 -> x0, waiting for transfers between devices: 288 us -> none  [forward_layer(): lax.psum(jnp.dot(mixed_heads, wout, preferred_element_type=jnp.float32),...]
    all_gather x0 -> x5, waiting for transfers between devices: none -> 275 us  [forward_layer(): lax.all_gather(jnp.dot(mixed_heads, wout, preferred_element_type=jnp.floa...]
    unnamed x786 -> x780, local copies, waits for them, and re-layouts: 74.9 us -> 67.8 us
where the time goes in v1:
time: 2720 us; the launch traced here: 2710 us
  waiting for transfers between devices  1370 us (50%)
  blocking collectives  481 us (18%)
  local copies, waits for them, and re-layouts  385 us (14%)
  matrix products  265 us (10%)
  other arithmetic  148 us (5%)
  starting transfers between devices  39.8 us (1%)
    all_gather x5, waiting for transfers between devices, forward_layer(): lax.all_gather(jnp.dot(mixed_heads, wout, preferred_element_type=jnp.floa...  275 us
    psum x5, waiting for transfers between devices, backward_layer(): lax.psum(jnp.einsum('irc,idc->rd', grad_projected, wqkv, preferred_elemen...  257 us
    all_to_all x5, blocking collectives, forward_layer(): lax.all_to_all(sent_rows, 'expert', split_axis=1, concat_axis=1, tiled=True)  207 us
    reduce_scatter x5, waiting for transfers between devices, forward_layer(): lax.psum_scatter(partial_value, 'tensor', scatter_dimension=2, tiled=True)  203 us
    reduce_scatter x5, waiting for transfers between devices, backward_layer(): lax.psum_scatter(row_terms, 'tensor', scatter_dimension=2, tiled=True)  174 us
    all_gather x5, waiting for transfers between devices, backward_layer(): grad_arrived = lax.all_gather(arrived_part, 'tensor', axis=2, tiled=True)  145 us
    all_gather x5, waiting for transfers between devices, backward_layer(): lax.all_gather(home_part, 'tensor', axis=2, tiled=True)  123 us
    all_to_all x5, blocking collectives, backward_layer(): lax.all_to_all(grad_sent.reshape(exp_dev, owners * capacity, quarter), 'e...  95.4 us
  transfers between devices with their start and end apart: 49, of which 43 were waited for; matrix products, arithmetic and copies ran while one was open for 12% of the time, Pallas kernels for 0%

profile of v1, /device:TPU:0, one launch (start us, length us, event | category | flops | bytes accessed | tf_op | source)
XLA Modules:
  0.0 2708.0 jit_solution(5512992514575595094)
XLA Ops:
  44.8 51.9 %all-gather.61.cloned.1.call-done = f32[4,394,768]{2,1,0:T(8,128)} async-done(((f32[1,394,768]{2,1,0:T(8,128)}), f32[4,394,768]{2,1,0:T(8,128)}) %all-gather.61.cloned.1.call-update) | async-done | bytes 4841488 | tf_op jit(solution)/shard_map/all_gather | solution.py:83
  117.9 41.5 %all_to_all.100 = bf16[2,512,768]{2,0,1:T(2,128)(2,1)} all-to-all(bf16[2,512,768]{2,0,1:T(2,128)(2,1)S(1)} %copy.1223), channel_id=1, replica_groups=mesh['section'=2,'expert'=4,'tensor'=4] {'expert'}, dimensions={1} | all-to-all | bytes 3145728 | tf_op jit(solution)/shard_map/all_to_all | solution.py:98
  282.2 55.6 %all-gather.63.cloned.1.call-done = f32[4,394,768]{2,1,0:T(8,128)} async-done(((f32[1,394,768]{2,1,0:T(8,128)}), f32[4,394,768]{2,1,0:T(8,128)}) %all-gather.63.cloned.1.call-update) | async-done | bytes 4841488 | tf_op jit(solution)/shard_map/all_gather | solution.py:83
  351.3 41.3 %all_to_all.101 = bf16[2,512,768]{2,0,1:T(2,128)(2,1)} all-to-all(bf16[2,512,768]{2,0,1:T(2,128)(2,1)S(1)} %copy.1240), channel_id=1, replica_groups=mesh['section'=2,'expert'=4,'tensor'=4] {'expert'}, dimensions={1} | all-to-all | bytes 3145728 | tf_op jit(solution)/shard_map/all_to_all | solution.py:98
  407.5 42.2 %reduce-scatter.13.cloned.1.call-done = f32[2,512,192]{1,2,0:T(8,128)} async-done(((f32[2,512,768]{1,2,0:T(8,128)}), f32[2,512,192]{1,2,0:T(8,128)}) %reduce-scatter.13.cloned.1.call-update) | async-done | bytes 786448 | tf_op jit(solution)/shard_map/reduce_scatter | solution.py:102
  521.0 55.5 %all-gather.65.cloned.1.call-done = f32[4,394,768]{2,1,0:T(8,128)} async-done(((f32[1,394,768]{2,1,0:T(8,128)}), f32[4,394,768]{2,1,0:T(8,128)}) %all-gather.65.cloned.1.call-update) | async-done | bytes 4841488 | tf_op jit(solution)/shard_map/all_gather | solution.py:83
  587.3 41.7 %all_to_all.102 = bf16[2,512,768]{2,0,1:T(2,128)(2,1)} all-to-all(bf16[2,512,768]{2,0,1:T(2,128)(2,1)S(1)} %copy.1258), channel_id=1, replica_groups=mesh['section'=2,'expert'=4,'tensor'=4] {'expert'}, dimensions={1} | all-to-all | bytes 3145728 | tf_op jit(solution)/shard_map/all_to_all | solution.py:98
  644.0 42.2 %reduce-scatter.15.cloned.1.call-done = f32[2,512,192]{1,2,0:T(8,128)} async-done(((f32[2,512,768]{1,2,0:T(8,128)}), f32[2,512,192]{1,2,0:T(8,128)}) %reduce-scatter.15.cloned.1.call-update) | async-done | bytes 786448 | tf_op jit(solution)/shard_map/reduce_scatter | solution.py:102
  736.4 55.8 %all-gather.67.cloned.1.call-done = f32[4,394,768]{2,1,0:T(8,128)} async-done(((f32[1,394,768]{2,1,0:T(8,128)}), f32[4,394,768]{2,1,0:T(8,128)}) %all-gather.67.cloned.1.call-update) | async-done | bytes 4841488 | tf_op jit(solution)/shard_map/all_gather | solution.py:83
  803.1 41.3 %all_to_all.103 = bf16[2,512,768]{2,0,1:T(2,128)(2,1)} all-to-all(bf16[2,512,768]{2,0,1:T(2,128)(2,1)S(1)} %copy.1276), channel_id=1, replica_groups=mesh['section'=2,'expert'=4,'tensor'=4] {'expert'}, dimensions={1} | all-to-all | bytes 3145728 | tf_op jit(solution)/shard_map/all_to_all | solution.py:98
  859.3 42.2 %reduce-scatter.17.cloned.1.call-done = f32[2,512,192]{1,2,0:T(8,128)} async-done(((f32[2,512,768]{1,2,0:T(8,128)}), f32[2,512,192]{1,2,0:T(8,128)}) %reduce-scatter.17.cloned.1.call-update) | async-done | bytes 786448 | tf_op jit(solution)/shard_map/reduce_scatter | solution.py:102
  948.5 55.9 %all-gather.69.cloned.1.call-done = f32[4,394,768]{2,1,0:T(8,128)} async-done(((f32[1,394,768]{2,1,0:T(8,128)}), f32[4,394,768]{2,1,0:T(8,128)}) %all-gather.69.cloned.1.call-update) | async-done | bytes 4841488 | tf_op jit(solution)/shard_map/all_gather | solution.py:83
  1015.3 41.3 %all_to_all.104 = bf16[2,512,768]{2,0,1:T(2,128)(2,1)} all-to-all(bf16[2,512,768]{2,0,1:T(2,128)(2,1)S(1)} %copy.1292), channel_id=1, replica_groups=mesh['section'=2,'expert'=4,'tensor'=4] {'expert'}, dimensions={1} | all-to-all | bytes 3145728 | tf_op jit(solution)/shard_map/all_to_all | solution.py:98
  1070.0 42.1 %reduce-scatter.19.cloned.1.call-done = f32[2,512,192]{1,2,0:T(8,128)} async-done(((f32[2,512,768]{1,2,0:T(8,128)}), f32[2,512,192]{1,2,0:T(8,128)}) %reduce-scatter.19.cloned.1.call-update) | async-done | bytes 786448 | tf_op jit(solution)/shard_map/reduce_scatter | solution.py:102
  1243.7 44.0 %reduce-scatter.21.cloned.1.call-done = f32[2,512,192]{1,2,0:T(8,128)} async-done(((f32[2,512,768]{1,2,0:T(8,128)}), f32[2,512,192]{1,2,0:T(8,128)}) %reduce-scatter.21.cloned.1.call-update) | async-done | bytes 786448 | tf_op jit(solution)/shard_map/reduce_scatter | solution.py:187
  1359.5 60.8 %all-reduce.9.cloned.1.call-done = f32[394,768]{0,1:T(8,128)} async-done(((f32[394,768]{0,1:T(8,128)}), f32[394,768]{0,1:T(8,128)}) %all-reduce.9.cloned.1.call-update) | async-done | bytes 1210384 | tf_op jit(solution)/shard_map/psum | solution.py:247
  1495.4 43.4 %reduce-scatter.23.cloned.1.call-done = f32[2,512,192]{1,2,0:T(8,128)} async-done(((f32[2,512,768]{1,2,0:T(8,128)}), f32[2,512,192]{1,2,0:T(8,128)}) %reduce-scatter.23.cloned.1.call-update) | async-done | bytes 786448 | tf_op jit(solution)/shard_map/reduce_scatter | solution.py:187
  1644.0 52.6 %all-reduce.11.cloned.1.call-done = f32[394,768]{0,1:T(8,128)} async-done(((f32[394,768]{0,1:T(8,128)}), f32[394,768]{0,1:T(8,128)}) %all-reduce.11.cloned.1.call-update) | async-done | bytes 1210384 | tf_op jit(solution)/shard_map/psum | solution.py:247
  1772.4 43.3 %reduce-scatter.25.cloned.1.call-done = f32[2,512,192]{1,2,0:T(8,128)} async-done(((f32[2,512,768]{1,2,0:T(8,128)}), f32[2,512,192]{1,2,0:T(8,128)}) %reduce-scatter.25.cloned.1.call-update) | async-done | bytes 786448 | tf_op jit(solution)/shard_map/reduce_scatter | solution.py:187
  1920.6 52.5 %all-reduce.13.cloned.1.call-done = f32[394,768]{0,1:T(8,128)} async-done(((f32[394,768]{0,1:T(8,128)}), f32[394,768]{0,1:T(8,128)}) %all-reduce.13.cloned.1.call-update) | async-done | bytes 1210384 | tf_op jit(solution)/shard_map/psum | solution.py:247
  2048.8 43.3 %reduce-scatter.27.cloned.1.call-done = f32[2,512,192]{1,2,0:T(8,128)} async-done(((f32[2,512,768]{1,2,0:T(8,128)}), f32[2,512,192]{1,2,0:T(8,128)}) %reduce-scatter.27.cloned.1.call-update) | async-done | bytes 786448 | tf_op jit(solution)/shard_map/reduce_scatter | solution.py:187
  2202.7 49.9 %all-reduce.15.cloned.1.call-done = f32[394,768]{0,1:T(8,128)} async-done(((f32[394,768]{0,1:T(8,128)}), f32[394,768]{0,1:T(8,128)}) %all-reduce.15.cloned.1.call-update) | async-done | bytes 1210384 | tf_op jit(solution)/shard_map/psum | solution.py:247
  2556.9 41.4 %all-reduce.17.cloned.1.call-done = f32[394,768]{0,1:T(8,128)} async-done(((f32[394,768]{0,1:T(8,128)}), f32[394,768]{0,1:T(8,128)}) %all-reduce.17.cloned.1.call-update) | async-done | bytes 1210384 | tf_op jit(solution)/shard_map/psum | solution.py:247
  2651.4 45.9 %all-reduce.19.cloned.1.call-done = (f32[1,3,768,192]{2,3,1,0:T(8,128)}, f32[1,192,768]{2,1,0:T(8,128)}) async-done(((f32[1,3,768,192]{2,3,1,0:T(8,128)}, f32[1,192,768]{2,1,0:T(8,128)}), (f32[1,3,768,192]{2,3,1,0:T(8,128)}, f32[1,192,768]{2,1,0:T(8,128)})) %all-reduce.19.cloned.1.call-update) | async-done | bytes 2359312 | tf_op jit(solution)/shard_map/psum | solution.py:360
  (1453 shorter events, 1560.4 us)
Async XLA Ops:
  35.2 179.6 %reduce-scatter.11.cloned.1.call-start = ((), (), s32[]{:S(2)}) async-start(), calls=%async_computation.30 | async-start | bytes 3932160 | tf_op jit(solution)/shard_map/reduce_scatter | solution.py:102
  221.7 116.2 %all-gather.63.cloned.1.call-start = ((), (), s32[]{:S(2)}) async-start(), calls=%async_computation.61 | async-start | bytes 6144000 | tf_op jit(solution)/shard_map/all_gather | solution.py:83
  280.4 169.3 %reduce-scatter.13.cloned.1.call-start = ((), (), s32[]{:S(2)}) async-start(), calls=%async_computation.31 | async-start | bytes 3932160 | tf_op jit(solution)/shard_map/reduce_scatter | solution.py:102
  456.5 120.0 %all-gather.65.cloned.1.call-start = ((), (), s32[]{:S(2)}) async-start(), calls=%async_computation.62 | async-start | bytes 6144000 | tf_op jit(solution)/shard_map/all_gather | solution.py:83
  519.0 167.2 %reduce-scatter.15.cloned.1.call-start = ((), (), s32[]{:S(2)}) async-start(), calls=%async_computation.32 | async-start | bytes 3932160 | tf_op jit(solution)/shard_map/reduce_scatter | solution.py:102
  693.1 99.2 %all-gather.67.cloned.1.call-start = ((), (), s32[]{:S(2)}) async-start(), calls=%async_computation.63 | async-start | bytes 6144000 | tf_op jit(solution)/shard_map/all_gather | solution.py:83
  734.9 166.5 %reduce-scatter.17.cloned.1.call-start = ((), (), s32[]{:S(2)}) async-start(), calls=%async_computation.33 | async-start | bytes 3932160 | tf_op jit(solution)/shard_map/reduce_scatter | solution.py:102
  947.2 165.0 %reduce-scatter.19.cloned.1.call-start = ((), (), s32[]{:S(2)}) async-start(), calls=%async_computation.34 | async-start | bytes 3932160 | tf_op jit(solution)/shard_map/reduce_scatter | solution.py:102
  1070.0 109.9 %all-gather.35.cloned.1.call-start = ((), (), s32[]{:S(2)}) async-start(), calls=%async_computation.38 | async-start | bytes 3932160 | tf_op jit(solution)/shard_map/all_gather | solution.py:114
  1309.8 110.5 %all-reduce.9.cloned.1.call-start = ((), (), s32[]{:S(2)}) async-start(), calls=%async_computation.39 | async-start | bytes 3145728 | tf_op jit(solution)/shard_map/psum | solution.py:247
  1359.4 125.6 %all-gather.37.cloned.1.call-start = ((), (), s32[]{:S(2)}) async-start(), calls=%async_computation.40 | async-start | bytes 1966080 | tf_op jit(solution)/shard_map/all_gather | solution.py:175
  1495.4 122.3 %all-gather.39.cloned.1.call-start = ((), (), s32[]{:S(2)}) async-start(), calls=%async_computation.42 | async-start | bytes 1966080 | tf_op jit(solution)/shard_map/all_gather | solution.py:191
  1561.0 135.7 %all-reduce.11.cloned.1.call-start = ((), (), s32[]{:S(2)}) async-start(), calls=%async_computation.44 | async-start | bytes 3145728 | tf_op jit(solution)/shard_map/psum | solution.py:247
  1635.8 126.0 %all-gather.43.cloned.1.call-start = ((), (), s32[]{:S(2)}) async-start(), calls=%async_computation.45 | async-start | bytes 1966080 | tf_op jit(solution)/shard_map/all_gather | solution.py:175
  1772.3 122.2 %all-gather.45.cloned.1.call-start = ((), (), s32[]{:S(2)}) async-start(), calls=%async_computation.47 | async-start | bytes 1966080 | tf_op jit(solution)/shard_map/all_gather | solution.py:191
  1837.8 135.3 %all-reduce.13.cloned.1.call-start = ((), (), s32[]{:S(2)}) async-start(), calls=%async_computation.49 | async-start | bytes 3145728 | tf_op jit(solution)/shard_map/psum | solution.py:247
  1912.2 126.0 %all-gather.49.cloned.1.call-start = ((), (), s32[]{:S(2)}) async-start(), calls=%async_computation.50 | async-start | bytes 1966080 | tf_op jit(solution)/shard_map/all_gather | solution.py:175
  2048.7 122.3 %all-gather.51.cloned.1.call-start = ((), (), s32[]{:S(2)}) async-start(), calls=%async_computation.52 | async-start | bytes 1966080 | tf_op jit(solution)/shard_map/all_gather | solution.py:191
  2114.1 138.5 %all-reduce.15.cloned.1.call-start = ((), (), s32[]{:S(2)}) async-start(), calls=%async_computation.54 | async-start | bytes 3145728 | tf_op jit(solution)/shard_map/psum | solution.py:247
  2191.7 133.5 %all-gather.55.cloned.1.call-start = ((), (), s32[]{:S(2)}) async-start(), calls=%async_computation.55 | async-start | bytes 1966080 | tf_op jit(solution)/shard_map/all_gather | solution.py:175
  2296.2 163.6 %reduce-scatter.29.cloned.1.call-start = ((), (), s32[]{:S(2)}) async-start(), calls=%async_computation.56 | async-start | bytes 3932160 | tf_op jit(solution)/shard_map/reduce_scatter | solution.py:187
  2335.1 149.0 %all-gather.59.cloned.1.call-start = ((), (), s32[]{:S(2)}) async-start(), calls=%async_computation.58 | async-start | bytes 3932160 | tf_op jit(solution)/shard_map/all_gather | solution.py:114
  2484.0 114.2 %all-reduce.17.cloned.1.call-start = ((), (), s32[]{:S(2)}) async-start(), calls=%async_computation.59 | async-start | bytes 3145728 | tf_op jit(solution)/shard_map/psum | solution.py:247
  2537.4 159.9 %all-reduce.19.cloned.1.call-start = ((), (), s32[]{:S(2)}) async-start(), calls=%async_computation.65 | async-start | bytes 4718592 | tf_op jit(solution)/shard_map/psum | solution.py:360
  (402 other events, 8255.6 us)
Sparse Core Ops, SparseCore 0:
  35.3 61.2 all-gather.60
  172.7 42.0 reduce-scatter.10
  280.5 57.2 all-gather.62
  407.6 42.0 reduce-scatter.12
  519.1 57.3 all-gather.64
  644.1 42.0 reduce-scatter.14
  735.1 57.1 all-gather.66
  859.4 42.0 reduce-scatter.16
  947.3 57.1 all-gather.68
  1243.8 43.8 reduce-scatter.20
  1359.5 60.7 all-reduce.8
  1494.9 43.8 reduce-scatter.22
  1540.5 43.8 all-gather.40
  1635.9 60.7 all-reduce.10
  1771.7 43.8 reduce-scatter.24
  1817.5 43.8 all-gather.46
  1912.3 60.7 all-reduce.12
  2048.1 43.8 reduce-scatter.26
  2093.9 43.8 all-gather.52
  2191.8 60.7 all-reduce.14
  2335.2 43.8 reduce-scatter.28
  2380.8 45.9 all-gather.58
  2537.5 60.7 all-reduce.16
  2601.1 96.1 all-reduce.18
  (12 shorter events, 381.0 us)
